TPU v7x, 128 devices: a whole 4x4x4 slice. The times are simulated.
128 devices in a mesh: row: 8 (over x, z_lo), col: 16 (over z_hi, y, core).
Axes of the slice: x: 4, y: 4, z: 4 (z_hi: 2, z_lo: 2; z = z_hi * 2 + z_lo), core: 2. Of those that a mesh axis runs over, the one named last changes fastest.
Arguments:
- factor_tiles: float32 [16, 1024, 8, 2048], P(None, 'row', None, 'col'), may hold values from -40 to 40, as said below
Outputs:
- rotated: float32 [16384, 16384], P(None, ('row', 'col'))
Inputs may be any that keep to these rules, and one draw needn't show every extreme that they name: `factor_tiles`: upper triangular: entries below the diagonal are zero, entries on it are positive.
All inputs are finite; a program needn't handle non-finite values.
Results may differ from a plain program's by a relative error of at most 0.0003.
Values sent between devices are 32-bit elements; how exact they have to be, the bound alone decides.
A program may use at most 128 MiB of HBM per device.

v0:
```python
import jax
import jax.numpy as jnp
from jax import lax
from jax.sharding import PartitionSpec as P
from jax.experimental import pallas as pl
from jax.experimental.pallas import tpu as pltpu

MESH = pl.DeviceIdType.MESH

LOGB = 7
OUTER = 4
INNER = 8
CHUNKS = 2


damping_ratio = 0.01
highest = lax.Precision.HIGHEST


def passed_along(value, axis, steps):
    count = lax.axis_size(axis)
    leading, last = (max(0, -steps), min(count, count - steps))
    return lax.ppermute(value, axis, [(source, source + steps) for source in range(leading, last)])


def solve_kernel(g_ref, q_ref):
    order = g_ref.shape[0]
    gram_matrix = g_ref[...]
    rows = lax.broadcasted_iota(jnp.int32, (order, order), 0)
    cols = lax.broadcasted_iota(jnp.int32, (order, order), 1)
    identity = rows == cols
    accum = jnp.where(identity, 1.0, 0.0).astype(gram_matrix.dtype)
    lane_ids = lax.broadcasted_iota(jnp.int32, (8, order), 1)
    for inner_step in range(INNER):
        stride = 2 ** ((LOGB - 1 - inner_step) % LOGB)

        def lane_partner(value):
            lead = (lax.broadcasted_iota(jnp.int32, value.shape, 1) & stride) == 0
            ahead = pltpu.roll(value, order - stride, 1)
            behind = pltpu.roll(value, stride, 1)
            return jnp.where(lead, ahead, behind)

        def row_partner(value):
            lead = (lax.broadcasted_iota(jnp.int32, value.shape, 0) & stride) == 0
            ahead = pltpu.roll(value, order - stride, 0)
            behind = pltpu.roll(value, stride, 0)
            return jnp.where(lead, ahead, behind)

        lane_lead = (lane_ids & stride) == 0
        diagonal = jnp.broadcast_to(
            jnp.sum(jnp.where(identity, gram_matrix, 0.0), axis=0, keepdims=True), (8, order)
        )
        cross_tail = jnp.broadcast_to(
            jnp.sum(jnp.where(rows == (cols ^ stride), gram_matrix, 0.0), axis=0, keepdims=True),
            (8, order),
        )
        diag_other = lane_partner(diagonal)
        diag_p = jnp.where(lane_lead, diagonal, diag_other)
        diag_q = jnp.where(lane_lead, diag_other, diagonal)
        cross = jnp.where(lane_lead, lane_partner(cross_tail), cross_tail)
        diag_gap = diag_q - diag_p
        diag_sum = diag_p + diag_q
        rot_angle = 0.5 * jnp.arctan2(
            2.0 * cross * diag_gap, diag_gap * diag_gap + damping_ratio * diag_sum * diag_sum
        )
        cosine = jnp.cos(rot_angle)
        sine_val = jnp.sin(rot_angle)
        signed_sine = jnp.where(lane_lead, -sine_val, sine_val)
        cos_lane = jnp.broadcast_to(cosine[:1], (order, order))
        sin_lane = jnp.broadcast_to(signed_sine[:1], (order, order))
        cos_row = jnp.sum(jnp.where(identity, cos_lane, 0.0), axis=1, keepdims=True)
        sin_row = jnp.sum(jnp.where(identity, sin_lane, 0.0), axis=1, keepdims=True)
        gram_matrix = cos_lane * gram_matrix + sin_lane * lane_partner(gram_matrix)
        gram_matrix = cos_row * gram_matrix + sin_row * row_partner(gram_matrix)
        accum = cos_lane * accum + sin_lane * lane_partner(accum)
    q_ref[...] = accum


def inner_solve(gram_matrix):
    return pl.pallas_call(
        solve_kernel,
        out_shape=jax.ShapeDtypeStruct(gram_matrix.shape, gram_matrix.dtype),
    )(gram_matrix)


def relayout(tile_work):
    cycles, row_count, tile_count, tile_width = tile_work.shape
    split_view = tile_work.reshape(cycles, 1, row_count, tile_count, tile_width)
    received = lax.all_to_all(split_view, "row", split_axis=3, concat_axis=1, tiled=True)
    return received.reshape(cycles * received.shape[1] * row_count, tile_width)


def gather_kernel(src_ref, out_ref, land, send_sem, recv_sem, local_sem):
    cycles, height, tiles, width = src_ref.shape
    me_r = lax.axis_index("row")
    me_c = lax.axis_index("col")
    n_c = lax.axis_size("col")
    k_me = me_r * n_c + me_c

    barrier = pltpu.get_barrier_semaphore()
    for t in range(tiles):
        @pl.when(me_r != t)
        def _():
            pl.semaphore_signal(barrier, inc=1, device_id=(t, me_c), device_id_type=MESH)
    pl.semaphore_wait(barrier, tiles - 1)

    def rows_of(block):
        return land.at[pl.ds(pl.multiple_of(block * height, height), height)]

    sends = []
    for i in range(cycles):
        block = i * tiles + me_r
        local = pltpu.make_async_copy(src_ref.at[i, :, me_r, :], rows_of(block), local_sem.at[i])
        pl.when(block <= k_me)(local.start)
        for t in range(tiles):
            wanted = (block <= t * n_c + me_c) & (me_r != t)
            copy = pltpu.make_async_remote_copy(
                src_ref=src_ref.at[i, :, t, :],
                dst_ref=rows_of(block),
                send_sem=send_sem.at[t, i],
                recv_sem=recv_sem.at[me_r, i],
                device_id=(t, me_c),
                device_id_type=MESH,
            )
            pl.when(wanted)(copy.start)
            sends.append((wanted, copy))
    for i in range(cycles):
        for r in range(tiles):
            block = i * tiles + r
            columns = slice(block * height, (block + 1) * height)
            incoming = pltpu.make_async_remote_copy(
                src_ref=src_ref.at[i, :, r, :],
                dst_ref=land.at[columns],
                send_sem=send_sem.at[r, i],
                recv_sem=recv_sem.at[r, i],
                device_id=(r, me_c),
                device_id_type=MESH,
            )
            local = pltpu.make_async_copy(src_ref.at[i, :, r, :], land.at[columns], local_sem.at[i])
            pl.when((block <= k_me) & (me_r != r))(incoming.wait_recv)
            pl.when((block <= k_me) & (me_r == r))(local.wait)

            @pl.when(block <= k_me)
            def _():
                out_ref[:, columns] = land[columns, :].T

            @pl.when(block > k_me)
            def _():
                out_ref[:, columns] = jnp.zeros((width, height), out_ref.dtype)

    for wanted, copy in sends:
        pl.when(wanted)(copy.wait_send)


def gather_columns(factor_tiles):
    cycles, height, tiles, width = factor_tiles.shape
    return pl.pallas_call(
        gather_kernel,
        out_shape=jax.ShapeDtypeStruct((width, cycles * tiles * height), factor_tiles.dtype),
        in_specs=[pl.BlockSpec(memory_space=pl.ANY)],
        out_specs=pl.BlockSpec(memory_space=pltpu.VMEM),
        scratch_shapes=[
            pltpu.VMEM((cycles * tiles * height, width), factor_tiles.dtype),
            pltpu.SemaphoreType.DMA((tiles, cycles)),
            pltpu.SemaphoreType.DMA((tiles, cycles)),
            pltpu.SemaphoreType.DMA((cycles,)),
        ],
        compiler_params=pltpu.CompilerParams(
            collective_id=0, has_side_effects=True, vmem_limit_bytes=48 * 1024 * 1024
        ),
    )(factor_tiles)


def summed(parts):
    total = parts[0]
    for part in parts[1:]:
        total = total + part
    return total


def per_device(factor_tiles):
    half_width = factor_tiles.shape[-1] // 2
    column_lines = gather_columns(factor_tiles)
    rows = column_lines.shape[1]
    span = rows // CHUNKS
    position = lax.axis_index(("row", "col"))
    devices_total = lax.axis_size(("row", "col"))
    first = position == 0
    last = position == devices_total - 1
    pieces = [column_lines[:, j * span:(j + 1) * span] for j in range(CHUNKS)]
    gram_matrix = jnp.einsum("in,jn->ij", column_lines, column_lines, precision=highest)
    rotation = inner_solve(gram_matrix)
    lines = [jnp.einsum("in,ij->jn", piece, rotation, precision=highest) for piece in pieces]
    for round_index in range(1, OUTER):
        fresh = []
        for piece in lines:
            top_half = piece[:half_width]
            bottom_half = piece[half_width:]
            outgoing = jnp.where(first, bottom_half, top_half)
            arrived = passed_along(outgoing, ("row", "col"), 1)
            behind = passed_along(bottom_half, ("row", "col"), -1)
            new_top = jnp.where(first, top_half, arrived)
            new_bottom = jnp.where(last, top_half, behind)
            fresh.append(jnp.concatenate([new_top, new_bottom], axis=0))
        gram_matrix = summed(
            [jnp.einsum("in,jn->ij", piece, piece, precision=highest) for piece in fresh]
        )
        rotation = inner_solve(gram_matrix)
        if round_index + 1 < OUTER:
            lines = [jnp.einsum("in,ij->jn", piece, rotation, precision=highest) for piece in fresh]
        else:
            whole = jnp.concatenate(fresh, axis=1)
            return jnp.einsum("in,ij->nj", whole, rotation, precision=highest)


def solution(mesh):
    return jax.shard_map(
        per_device,
        mesh=mesh,
        in_specs=(P(None, "row", None, "col"),),
        out_specs=P(None, ("row", "col")),
        check_vma=False,
    )
```

profile of v0, /device:TPU:63, one launch (start us, length us, event | category | flops | bytes accessed | tf_op | source)
XLA Modules:
  0.0 362.4 jit_solution(1919582018443980062)
XLA Ops:
  0.0 93.5 %shard_map.17 = f32[128,16384]{1,0:T(8,128)} custom-call(f32[16,128,8,128]{3,2,1,0:T(8,128)} %src_ref.1), custom_call_target="tpu_custom_call" | custom-call | tf_op jit(solution)/shard_map/pallas_call | solution.py:157
  93.5 11.1 %fusion.44.g_ref = f32[128,128]{1,0:T(8,128)} fusion(f32[128,16384]{1,0:T(8,128)} %shard_map.17), kind=kOutput, calls=%fused_computation.64 | convolution fusion | flops 3221225472 | bytes 8454144 | tf_op jit(solution)/shard_map/in,jn->ij/dot_general | solution.py:191
  104.6 4.7 %shard_map.18 = f32[128,128]{1,0:T(8,128)} custom-call(f32[128,128]{1,0:T(8,128)} %fusion.44.g_ref), custom_call_target="tpu_custom_call" | custom-call | tf_op jit(solution)/shard_map/pallas_call | solution.py:80
  109.3 8.0 %fusion.16 = f32[128,8192]{1,0:T(8,128)} fusion(f32[128,128]{1,0:T(8,128)} %shard_map.18, f32[128,16384]{1,0:T(8,128)} %shard_map.17), kind=kOutput, calls=%fused_computation.20 | convolution fusion | flops 1610612736 | bytes 8454144 | tf_op jit(solution)/shard_map/in,ij->jn/dot_general | solution.py:193
  117.3 4.9 %slice_select_fusion.14 = (f32[64,8192]{1,0:T(8,128)}, f32[64,8192]{1,0:T(8,128)}) fusion(f32[128,8192]{1,0:T(8,128)} %fusion.16, pred[]{:T(512)S(6)} %eq.6), kind=kLoop, calls=%fused_computation.46 | loop fusion | flops 524288 | bytes 8388609 | tf_op jit(solution)/shard_map/jit(_where)/select_n | solution.py:199
  122.2 7.4 %collective-permute-start.2 = (f32[64,8192]{1,0:T(8,128)}, f32[64,8192]{1,0:T(8,128)S(1)}, u32[]{:S(2)}, u32[]{:S(2)}) collective-permute-start(f32[64,8192]{1,0:T(8,128)} %get-tuple-element.27), channel_id=1, source_target_pairs={{0,1},{1,2},{2,3},{3,4},{4,5},{5,6},{6,7},{7,8},{8,9},{9,10},{10,1... | collective-permute-start | bytes 6291464 | tf_op jit(solution)/shard_map/ppermute | solution.py:23
  138.7 7.2 %collective-permute-start = (f32[64,8192]{1,0:T(8,128)}, f32[64,8192]{1,0:T(8,128)}, u32[]{:S(2)}, u32[]{:S(2)}) collective-permute-start(f32[64,8192]{1,0:T(8,128)} %get-tuple-element.23), channel_id=1, source_target_pairs={{0,1},{1,2},{2,3},{3,4},{4,5},{5,6},{6,7},{7,8},{8,9},{9,10},{10,1... | collective-permute-start | bytes 6291464 | tf_op jit(solution)/shard_map/ppermute | solution.py:23
  145.9 10.7 %collective-permute-start.1 = (f32[64,8192]{1,0:T(8,128)}, f32[64,8192]{1,0:T(8,128)}, u32[]{:S(2)}, u32[]{:S(2)}) collective-permute-start(f32[64,8192]{1,0:T(8,128)} %get-tuple-element.24), channel_id=1, source_target_pairs={{1,0},{2,1},{3,2},{4,3},{5,4},{6,5},{7,6},{8,7},{9,8},{10,9},{11,1... | collective-permute-start | bytes 6291464 | tf_op jit(solution)/shard_map/ppermute | solution.py:23
  167.6 7.8 %collective-permute-done = f32[64,8192]{1,0:T(8,128)} collective-permute-done((f32[64,8192]{1,0:T(8,128)}, f32[64,8192]{1,0:T(8,128)}, u32[]{:S(2)}, u32[]{:S(2)}) %collective-permute-start) | collective-permute-done | bytes 2097184 | tf_op jit(solution)/shard_map/ppermute | solution.py:23
  175.4 8.0 %collective-permute-done.1 = f32[64,8192]{1,0:T(8,128)} collective-permute-done((f32[64,8192]{1,0:T(8,128)}, f32[64,8192]{1,0:T(8,128)}, u32[]{:S(2)}, u32[]{:S(2)}) %collective-permute-start.1) | collective-permute-done | bytes 2097184 | tf_op jit(solution)/shard_map/ppermute | solution.py:23
  192.3 4.7 %shard_map.19 = f32[128,128]{1,0:T(8,128)} custom-call(f32[128,128]{1,0:T(8,128)} %fusion.28.g_ref), custom_call_target="tpu_custom_call" | custom-call | tf_op jit(solution)/shard_map/pallas_call | solution.py:80
  197.0 5.9 %fusion.24 = f32[128,8192]{1,0:T(8,128)S(1)} fusion(f32[128,128]{1,0:T(8,128)} %shard_map.19, f32[64,8192]{1,0:T(8,128)} %copy-done.3, f32[64,8192]{1,0:T(8,128)S(1)} %get-tuple-element.25), kind=kOutput, calls=%fused_computation.28 | convolution fusion | flops 1611661312 | bytes 8454144 | tf_op jit(solution)/shard_map/in,ij->jn/dot_general | solution.py:210
  212.4 6.8 %collective-permute-start.4 = (f32[64,8192]{1,0:T(8,128)S(1)}, f32[64,8192]{1,0:T(8,128)S(1)}, u32[]{:S(2)}, u32[]{:S(2)}) collective-permute-start(f32[64,8192]{1,0:T(8,128)S(1)} %get-tuple-element.15), channel_id=1, source_target_pairs={{0,1},{1,2},{2,3},{3,4},{4,5},{5,6},{6,7},{7,8},{8,9},{9,10},{10,1... | collective-permute-start | bytes 6291464 | tf_op jit(solution)/shard_map/ppermute | solution.py:23
  221.5 7.0 %collective-permute-done.6 = f32[64,8192]{1,0:T(8,128)S(1)} collective-permute-done((f32[64,8192]{1,0:T(8,128)S(1)}, f32[64,8192]{1,0:T(8,128)S(1)}, u32[]{:S(2)}, u32[]{:S(2)}) %collective-permute-start.6) | collective-permute-done | bytes 2097184 | tf_op jit(solution)/shard_map/ppermute | solution.py:23
  228.5 8.0 %collective-permute-done.7 = f32[64,8192]{1,0:T(8,128)S(1)} collective-permute-done((f32[64,8192]{1,0:T(8,128)S(1)}, f32[64,8192]{1,0:T(8,128)S(1)}, u32[]{:S(2)}, u32[]{:S(2)}) %collective-permute-start.7) | collective-permute-done | bytes 2097184 | tf_op jit(solution)/shard_map/ppermute | solution.py:23
  240.3 10.6 %collective-permute-done.4 = f32[64,8192]{1,0:T(8,128)S(1)} collective-permute-done((f32[64,8192]{1,0:T(8,128)S(1)}, f32[64,8192]{1,0:T(8,128)S(1)}, u32[]{:S(2)}, u32[]{:S(2)}) %collective-permute-start.4) | collective-permute-done | bytes 2097184 | tf_op jit(solution)/shard_map/ppermute | solution.py:23
  251.0 8.0 %collective-permute-done.5 = f32[64,8192]{1,0:T(8,128)S(1)} collective-permute-done((f32[64,8192]{1,0:T(8,128)S(1)}, f32[64,8192]{1,0:T(8,128)S(1)}, u32[]{:S(2)}, u32[]{:S(2)}) %collective-permute-start.5) | collective-permute-done | bytes 2097184 | tf_op jit(solution)/shard_map/ppermute | solution.py:23
  270.3 5.8 %fusion.20 = f32[128,8192]{1,0:T(8,128)S(1)} fusion(f32[128,128]{1,0:T(8,128)} %shard_map.20, f32[64,8192]{1,0:T(8,128)} %copy-done.4, f32[64,8192]{1,0:T(8,128)S(1)} %get-tuple-element.17), kind=kOutput, calls=%fused_computation.24 | convolution fusion | flops 1611661312 | bytes 8454144 | tf_op jit(solution)/shard_map/in,ij->jn/dot_general | solution.py:210
  285.7 6.8 %collective-permute-start.8 = (f32[64,8192]{1,0:T(8,128)S(1)}, f32[64,8192]{1,0:T(8,128)S(1)}, u32[]{:S(2)}, u32[]{:S(2)}) collective-permute-start(f32[64,8192]{1,0:T(8,128)S(1)} %get-tuple-element.7), channel_id=1, source_target_pairs={{0,1},{1,2},{2,3},{3,4},{4,5},{5,6},{6,7},{7,8},{8,9},{9,10},{10,1... | collective-permute-start | bytes 6291464 | tf_op jit(solution)/shard_map/ppermute | solution.py:23
  294.6 7.2 %collective-permute-done.10 = f32[64,8192]{1,0:T(8,128)S(1)} collective-permute-done((f32[64,8192]{1,0:T(8,128)S(1)}, f32[64,8192]{1,0:T(8,128)S(1)}, u32[]{:S(2)}, u32[]{:S(2)}) %collective-permute-start.10) | collective-permute-done | bytes 2097184 | tf_op jit(solution)/shard_map/ppermute | solution.py:23
  301.7 8.0 %collective-permute-done.11 = f32[64,8192]{1,0:T(8,128)S(1)} collective-permute-done((f32[64,8192]{1,0:T(8,128)S(1)}, f32[64,8192]{1,0:T(8,128)S(1)}, u32[]{:S(2)}, u32[]{:S(2)}) %collective-permute-start.11) | collective-permute-done | bytes 2097184 | tf_op jit(solution)/shard_map/ppermute | solution.py:23
  313.6 10.6 %collective-permute-done.8 = f32[64,8192]{1,0:T(8,128)S(1)} collective-permute-done((f32[64,8192]{1,0:T(8,128)S(1)}, f32[64,8192]{1,0:T(8,128)S(1)}, u32[]{:S(2)}, u32[]{:S(2)}) %collective-permute-start.8) | collective-permute-done | bytes 2097184 | tf_op jit(solution)/shard_map/ppermute | solution.py:23
  324.2 8.0 %collective-permute-done.9 = f32[64,8192]{1,0:T(8,128)S(1)} collective-permute-done((f32[64,8192]{1,0:T(8,128)S(1)}, f32[64,8192]{1,0:T(8,128)S(1)}, u32[]{:S(2)}, u32[]{:S(2)}) %collective-permute-start.9) | collective-permute-done | bytes 2097184 | tf_op jit(solution)/shard_map/ppermute | solution.py:23
  343.5 18.7 %fusion = f32[16384,128]{1,0:T(8,128)} fusion(f32[128,128]{1,0:T(8,128)} %shard_map.21, f32[64,8192]{1,0:T(8,128)} %copy-done.13, f32[64,8192]{1,0:T(8,128)S(1)} %get-tuple-element.9, f32[64,8192]{1,0:T(8,128)} %copy-done.15, f32[64,8192]{1,0:T(8,128)} %copy-done.14), kind=kOutput, calls=%fused_computation | convolution fusion | flops 3227516928 | bytes 16842752 | tf_op jit(solution)/shard_map/in,ij->nj/dot_general | solution.py:213
  (71 shorter events, 82.2 us)
Async XLA Ops:
  109.3 22.3 %copy-start.17 = (f32[128,128]{1,0:T(8,128)S(1)}, f32[128,128]{1,0:T(8,128)}, u32[]{:S(2)}) copy-start(f32[128,128]{1,0:T(8,128)} %shard_map.18) | copy-start | bytes 196612
  117.3 14.3 %copy-start = (f32[128,16384]{1,0:T(8,128)S(1)}, f32[128,16384]{1,0:T(8,128)}, u32[]{:S(2)}) copy-start(f32[128,16384]{1,0:T(8,128)} %shard_map.17) | copy-start | bytes 25165828
  122.2 34.5 %collective-permute-start.2 = (f32[64,8192]{1,0:T(8,128)}, f32[64,8192]{1,0:T(8,128)S(1)}, u32[]{:S(2)}, u32[]{:S(2)}) collective-permute-start(f32[64,8192]{1,0:T(8,128)} %get-tuple-element.27), channel_id=1, source_target_pairs={{0,1},{1,2},{2,3},{3,4},{4,5},{5,6},{6,7},{7,8},{8,9},{9,10},{10,1... | collective-permute-start | bytes 6291464 | tf_op jit(solution)/shard_map/ppermute | solution.py:23
  129.7 31.3 %collective-permute-start.3 = (f32[64,8192]{1,0:T(8,128)}, f32[64,8192]{1,0:T(8,128)}, u32[]{:S(2)}, u32[]{:S(2)}) collective-permute-start(f32[64,8192]{1,0:T(8,128)} %get-tuple-element.28), channel_id=1, source_target_pairs={{1,0},{2,1},{3,2},{4,3},{5,4},{6,5},{7,6},{8,7},{9,8},{10,9},{11,1... | collective-permute-start | bytes 6291464 | tf_op jit(solution)/shard_map/ppermute | solution.py:23
  138.7 36.7 %collective-permute-start = (f32[64,8192]{1,0:T(8,128)}, f32[64,8192]{1,0:T(8,128)}, u32[]{:S(2)}, u32[]{:S(2)}) collective-permute-start(f32[64,8192]{1,0:T(8,128)} %get-tuple-element.23), channel_id=1, source_target_pairs={{0,1},{1,2},{2,3},{3,4},{4,5},{5,6},{6,7},{7,8},{8,9},{9,10},{10,1... | collective-permute-start | bytes 6291464 | tf_op jit(solution)/shard_map/ppermute | solution.py:23
  145.9 37.5 %collective-permute-start.1 = (f32[64,8192]{1,0:T(8,128)}, f32[64,8192]{1,0:T(8,128)}, u32[]{:S(2)}, u32[]{:S(2)}) collective-permute-start(f32[64,8192]{1,0:T(8,128)} %get-tuple-element.24), channel_id=1, source_target_pairs={{1,0},{2,1},{3,2},{4,3},{5,4},{6,5},{7,6},{8,7},{9,8},{10,9},{11,1... | collective-permute-start | bytes 6291464 | tf_op jit(solution)/shard_map/ppermute | solution.py:23
  164.2 3.4 copy-start.3
  164.2 19.3 %copy-start.2 = (f32[128,8192]{1,0:T(8,128)S(1)}, f32[128,8192]{1,0:T(8,128)}, u32[]{:S(2)}) copy-start(f32[128,8192]{1,0:T(8,128)} %copy-done.1) | copy-start | bytes 12582916
  202.9 5.1 %copy-start.6 = (f32[64,8192]{1,0:T(8,128)S(1)}, f32[64,8192]{1,0:T(8,128)}, u32[]{:S(2)}) copy-start(f32[64,8192]{1,0:T(8,128)} %copy-done.5) | copy-start | bytes 6291460
  202.9 5.1 %copy-start.8 = (f32[64,8192]{1,0:T(8,128)S(1)}, f32[64,8192]{1,0:T(8,128)}, u32[]{:S(2)}) copy-start(f32[64,8192]{1,0:T(8,128)} %copy-done.7) | copy-start | bytes 6291460
  202.9 5.1 %copy-start.18 = (f32[128,128]{1,0:T(8,128)S(1)}, f32[128,128]{1,0:T(8,128)}, u32[]{:S(2)}) copy-start(f32[128,128]{1,0:T(8,128)} %shard_map.19) | copy-start | bytes 196612
  203.3 25.1 %collective-permute-start.6 = (f32[64,8192]{1,0:T(8,128)S(1)}, f32[64,8192]{1,0:T(8,128)S(1)}, u32[]{:S(2)}, u32[]{:S(2)}) collective-permute-start(f32[64,8192]{1,0:T(8,128)S(1)} %get-tuple-element.19), channel_id=1, source_target_pairs={{0,1},{1,2},{2,3},{3,4},{4,5},{5,6},{6,7},{7,8},{8,9},{9,10},{10,1... | collective-permute-start | bytes 6291464 | tf_op jit(solution)/shard_map/ppermute | solution.py:23
  205.5 31.0 %collective-permute-start.7 = (f32[64,8192]{1,0:T(8,128)S(1)}, f32[64,8192]{1,0:T(8,128)S(1)}, u32[]{:S(2)}, u32[]{:S(2)}) collective-permute-start(f32[64,8192]{1,0:T(8,128)S(1)} %get-tuple-element.20), channel_id=1, source_target_pairs={{1,0},{2,1},{3,2},{4,3},{5,4},{6,5},{7,6},{8,7},{9,8},{10,9},{11,1... | collective-permute-start | bytes 6291464 | tf_op jit(solution)/shard_map/ppermute | solution.py:23
  212.4 38.5 %collective-permute-start.4 = (f32[64,8192]{1,0:T(8,128)S(1)}, f32[64,8192]{1,0:T(8,128)S(1)}, u32[]{:S(2)}, u32[]{:S(2)}) collective-permute-start(f32[64,8192]{1,0:T(8,128)S(1)} %get-tuple-element.15), channel_id=1, source_target_pairs={{0,1},{1,2},{2,3},{3,4},{4,5},{5,6},{6,7},{7,8},{8,9},{9,10},{10,1... | collective-permute-start | bytes 6291464 | tf_op jit(solution)/shard_map/ppermute | solution.py:23
  219.2 39.8 %collective-permute-start.5 = (f32[64,8192]{1,0:T(8,128)S(1)}, f32[64,8192]{1,0:T(8,128)S(1)}, u32[]{:S(2)}, u32[]{:S(2)}) collective-permute-start(f32[64,8192]{1,0:T(8,128)S(1)} %get-tuple-element.16), channel_id=1, source_target_pairs={{1,0},{2,1},{3,2},{4,3},{5,4},{6,5},{7,6},{8,7},{9,8},{10,9},{11,1... | collective-permute-start | bytes 6291464 | tf_op jit(solution)/shard_map/ppermute | solution.py:23
  236.9 3.4 copy-start.4
  276.1 5.1 %copy-start.10 = (f32[64,8192]{1,0:T(8,128)S(1)}, f32[64,8192]{1,0:T(8,128)}, u32[]{:S(2)}) copy-start(f32[64,8192]{1,0:T(8,128)} %copy-done.9) | copy-start | bytes 6291460
  276.1 5.1 %copy-start.12 = (f32[64,8192]{1,0:T(8,128)S(1)}, f32[64,8192]{1,0:T(8,128)}, u32[]{:S(2)}) copy-start(f32[64,8192]{1,0:T(8,128)} %copy-done.11) | copy-start | bytes 6291460
  276.1 5.1 %copy-start.19 = (f32[128,128]{1,0:T(8,128)S(1)}, f32[128,128]{1,0:T(8,128)}, u32[]{:S(2)}) copy-start(f32[128,128]{1,0:T(8,128)} %shard_map.20) | copy-start | bytes 196612
  276.6 25.1 %collective-permute-start.10 = (f32[64,8192]{1,0:T(8,128)S(1)}, f32[64,8192]{1,0:T(8,128)S(1)}, u32[]{:S(2)}, u32[]{:S(2)}) collective-permute-start(f32[64,8192]{1,0:T(8,128)S(1)} %get-tuple-element.11), channel_id=1, source_target_pairs={{0,1},{1,2},{2,3},{3,4},{4,5},{5,6},{6,7},{7,8},{8,9},{9,10},{10,1... | collective-permute-start | bytes 6291464 | tf_op jit(solution)/shard_map/ppermute | solution.py:23
  278.8 31.0 %collective-permute-start.11 = (f32[64,8192]{1,0:T(8,128)S(1)}, f32[64,8192]{1,0:T(8,128)S(1)}, u32[]{:S(2)}, u32[]{:S(2)}) collective-permute-start(f32[64,8192]{1,0:T(8,128)S(1)} %get-tuple-element.12), channel_id=1, source_target_pairs={{1,0},{2,1},{3,2},{4,3},{5,4},{6,5},{7,6},{8,7},{9,8},{10,9},{11,1... | collective-permute-start | bytes 6291464 | tf_op jit(solution)/shard_map/ppermute | solution.py:23
  285.7 38.5 %collective-permute-start.8 = (f32[64,8192]{1,0:T(8,128)S(1)}, f32[64,8192]{1,0:T(8,128)S(1)}, u32[]{:S(2)}, u32[]{:S(2)}) collective-permute-start(f32[64,8192]{1,0:T(8,128)S(1)} %get-tuple-element.7), channel_id=1, source_target_pairs={{0,1},{1,2},{2,3},{3,4},{4,5},{5,6},{6,7},{7,8},{8,9},{9,10},{10,1... | collective-permute-start | bytes 6291464 | tf_op jit(solution)/shard_map/ppermute | solution.py:23
  292.4 39.8 %collective-permute-start.9 = (f32[64,8192]{1,0:T(8,128)S(1)}, f32[64,8192]{1,0:T(8,128)S(1)}, u32[]{:S(2)}, u32[]{:S(2)}) collective-permute-start(f32[64,8192]{1,0:T(8,128)S(1)} %get-tuple-element.8), channel_id=1, source_target_pairs={{1,0},{2,1},{3,2},{4,3},{5,4},{6,5},{7,6},{8,7},{9,8},{10,9},{11,1... | collective-permute-start | bytes 6291464 | tf_op jit(solution)/shard_map/ppermute | solution.py:23
  310.1 3.4 copy-start.13
  (8 other events, 14.7 us)
where the time goes:
time: 368 us; the launch traced here: 362 us
  Pallas kernels  112 us (30%)
  waiting for transfers between devices  86.2 us (23%)
  matrix products  83.9 us (23%)
  starting transfers between devices  54.5 us (15%)
  other arithmetic  16.6 us (5%)
  local copies, waits for them, and re-layouts  8.15 us (2%)
    pallas_call x1, Pallas kernels, gather_columns(): pl.pallas_call(gather_kernel, out_shape=jax.ShapeDtypeStruct((width, cycl...  93.5 us
    ppermute x12, waiting for transfers between devices, passed_along(): lax.ppermute(value, axis, [(source, source + steps) for source in range(l...  86.2 us
    ppermute x12, starting transfers between devices, passed_along(): lax.ppermute(value, axis, [(source, source + steps) for source in range(l...  54.5 us
    dot_general x6, matrix products, per_device(): jnp.einsum('in,ij->jn', piece, rotation, precision=highest)  31.5 us
    dot_general x6, matrix products, per_device(): jnp.einsum('in,jn->ij', piece, piece, precision=highest)  22.6 us
    pallas_call x4, Pallas kernels, inner_solve(): pl.pallas_call(solve_kernel, out_shape=jax.ShapeDtypeStruct(gram_matrix.s...  18.9 us
    dot_general x1, matrix products, per_device(): return jnp.einsum('in,ij->nj', whole, rotation, precision=highest)  18.7 us
    dot_general x1, matrix products, per_device(): jnp.einsum('in,jn->ij', column_lines, column_lines, precision=highest)  11.1 us
  transfers between devices with their start and end apart: 12, of which 11 were waited for; matrix products, arithmetic and copies ran while one was open for 8% of the time, Pallas kernels for 0%

commit v1 on v0

--- a/solution.py
+++ b/solution.py
@@ -190,24 +190,28 @@
     pieces = [column_lines[:, j * span:(j + 1) * span] for j in range(CHUNKS)]
     gram_matrix = jnp.einsum("in,jn->ij", column_lines, column_lines, precision=highest)
     rotation = inner_solve(gram_matrix)
-    lines = [jnp.einsum("in,ij->jn", piece, rotation, precision=highest) for piece in pieces]
+    def sending(rotation):
+        return jnp.where(first, jnp.roll(rotation, half_width, axis=1), rotation)
+
+    lines = [jnp.einsum("in,ij->jn", piece, sending(rotation), precision=highest) for piece in pieces]
     for round_index in range(1, OUTER):
         fresh = []
         for piece in lines:
-            top_half = piece[:half_width]
-            bottom_half = piece[half_width:]
-            outgoing = jnp.where(first, bottom_half, top_half)
+            outgoing = piece[:half_width]
+            kept = piece[half_width:]
             arrived = passed_along(outgoing, ("row", "col"), 1)
-            behind = passed_along(bottom_half, ("row", "col"), -1)
-            new_top = jnp.where(first, top_half, arrived)
-            new_bottom = jnp.where(last, top_half, behind)
+            behind = passed_along(kept, ("row", "col"), -1)
+            new_top = jnp.where(first, kept, arrived)
+            new_bottom = jnp.where(last, outgoing, behind)
             fresh.append(jnp.concatenate([new_top, new_bottom], axis=0))
         gram_matrix = summed(
             [jnp.einsum("in,jn->ij", piece, piece, precision=highest) for piece in fresh]
         )
         rotation = inner_solve(gram_matrix)
         if round_index + 1 < OUTER:
-            lines = [jnp.einsum("in,ij->jn", piece, rotation, precision=highest) for piece in fresh]
+            lines = [
+                jnp.einsum("in,ij->jn", piece, sending(rotation), precision=highest) for piece in fresh
+            ]
         else:
             whole = jnp.concatenate(fresh, axis=1)
             return jnp.einsum("in,ij->nj", whole, rotation, precision=highest)

time: 368 us -> 370 us (level)
  local copies, waits for them, and re-layouts: 8.15 us -> 18.2 us
  other arithmetic: 16.6 us -> 11.5 us
    slice x0 -> x9, local copies, waits for them, and re-layouts: none -> 9.21 us  [the longest x6 6.23 us: per_device(): outgoing = piece[:half_width]]
    select_n x12 -> x9, other arithmetic: 16.6 us -> 11.5 us  [the longest x6 8.54 us: per_device(): new_top = jnp.where(first, kept, arrived)]
    unnamed x40 -> x38, local copies, waits for them, and re-layouts: 8.15 us -> 8.96 us
where the time goes in v1:
time: 370 us; the launch traced here: 364 us
  Pallas kernels  112 us (30%)
  waiting for transfers between devices  85.5 us (23%)
  matrix products  81.6 us (22%)
  starting transfers between devices  54.4 us (15%)
  local copies, waits for them, and re-layouts  18.2 us (5%)
  other arithmetic  11.5 us (3%)
    pallas_call x1, Pallas kernels, gather_columns(): pl.pallas_call(gather_kernel, out_shape=jax.ShapeDtypeStruct((width, cycl...  93.5 us
    ppermute x12, waiting for transfers between devices, passed_along(): lax.ppermute(value, axis, [(source, source + steps) for source in range(l...  85.5 us
    ppermute x12, starting transfers between devices, passed_along(): lax.ppermute(value, axis, [(source, source + steps) for source in range(l...  54.4 us
    dot_general x6, matrix products, per_device(): jnp.einsum('in,ij->jn', piece, sending(rotation), precision=highest)  29.2 us
    dot_general x6, matrix products, per_device(): jnp.einsum('in,jn->ij', piece, piece, precision=highest)  22.6 us
    pallas_call x4, Pallas kernels, inner_solve(): pl.pallas_call(solve_kernel, out_shape=jax.ShapeDtypeStruct(gram_matrix.s...  18.9 us
    dot_general x1, matrix products, per_device(): return jnp.einsum('in,ij->nj', whole, rotation, precision=highest)  18.7 us
    dot_general x1, matrix products, per_device(): jnp.einsum('in,jn->ij', column_lines, column_lines, precision=highest)  11.1 us
  transfers between devices with their start and end apart: 12, of which 11 were waited for; matrix products, arithmetic and copies ran while one was open for 8% of the time, Pallas kernels for 0%

profile of v1, /device:TPU:63, one launch (start us, length us, event | category | flops | bytes accessed | tf_op | source)
XLA Modules:
  0.0 364.2 jit_solution(10401150068499235554)
XLA Ops:
  0.0 93.5 %shard_map.17 = f32[128,16384]{1,0:T(8,128)} custom-call(f32[16,128,8,128]{3,2,1,0:T(8,128)} %src_ref.1), custom_call_target="tpu_custom_call" | custom-call | tf_op jit(solution)/shard_map/pallas_call | solution.py:157
  93.5 11.1 %fusion.53.g_ref = f32[128,128]{1,0:T(8,128)} fusion(f32[128,16384]{1,0:T(8,128)} %shard_map.17), kind=kOutput, calls=%fused_computation.70 | convolution fusion | flops 3221225472 | bytes 8454144 | tf_op jit(solution)/shard_map/in,jn->ij/dot_general | solution.py:191
  104.6 4.7 %shard_map.18 = f32[128,128]{1,0:T(8,128)} custom-call(f32[128,128]{1,0:T(8,128)} %fusion.53.g_ref), custom_call_target="tpu_custom_call" | custom-call | tf_op jit(solution)/shard_map/pallas_call | solution.py:80
  111.4 5.6 %fusion.16 = f32[128,8192]{1,0:T(8,128)S(1)} fusion(f32[128,128]{1,0:T(8,128)S(1)} %maximum_select_fusion, f32[128,16384]{1,0:T(8,128)} %shard_map.17), kind=kOutput, calls=%fused_computation.20 | convolution fusion | flops 1610612736 | bytes 8454144 | tf_op jit(solution)/shard_map/in,ij->jn/dot_general | solution.py:196
  120.4 7.3 %collective-permute-start.2 = (f32[64,8192]{1,0:T(8,128)}, f32[64,8192]{1,0:T(8,128)S(1)}, u32[]{:S(2)}, u32[]{:S(2)}) collective-permute-start(f32[64,8192]{1,0:T(8,128)} %get-tuple-element.27), channel_id=1, source_target_pairs={{0,1},{1,2},{2,3},{3,4},{4,5},{5,6},{6,7},{7,8},{8,9},{9,10},{10,1... | collective-permute-start | bytes 6291464 | tf_op jit(solution)/shard_map/ppermute | solution.py:23
  136.7 7.2 %collective-permute-start = (f32[64,8192]{1,0:T(8,128)}, f32[64,8192]{1,0:T(8,128)}, u32[]{:S(2)}, u32[]{:S(2)}) collective-permute-start(f32[64,8192]{1,0:T(8,128)} %get-tuple-element.23), channel_id=1, source_target_pairs={{0,1},{1,2},{2,3},{3,4},{4,5},{5,6},{6,7},{7,8},{8,9},{9,10},{10,1... | collective-permute-start | bytes 6291464 | tf_op jit(solution)/shard_map/ppermute | solution.py:23
  143.9 10.7 %collective-permute-start.1 = (f32[64,8192]{1,0:T(8,128)}, f32[64,8192]{1,0:T(8,128)}, u32[]{:S(2)}, u32[]{:S(2)}) collective-permute-start(f32[64,8192]{1,0:T(8,128)} %get-tuple-element.24), channel_id=1, source_target_pairs={{1,0},{2,1},{3,2},{4,3},{5,4},{6,5},{7,6},{8,7},{9,8},{10,9},{11,1... | collective-permute-start | bytes 6291464 | tf_op jit(solution)/shard_map/ppermute | solution.py:23
  166.3 7.1 %collective-permute-done = f32[64,8192]{1,0:T(8,128)} collective-permute-done((f32[64,8192]{1,0:T(8,128)}, f32[64,8192]{1,0:T(8,128)}, u32[]{:S(2)}, u32[]{:S(2)}) %collective-permute-start) | collective-permute-done | bytes 2097184 | tf_op jit(solution)/shard_map/ppermute | solution.py:23
  173.4 8.0 %collective-permute-done.1 = f32[64,8192]{1,0:T(8,128)} collective-permute-done((f32[64,8192]{1,0:T(8,128)}, f32[64,8192]{1,0:T(8,128)}, u32[]{:S(2)}, u32[]{:S(2)}) %collective-permute-start.1) | collective-permute-done | bytes 2097184 | tf_op jit(solution)/shard_map/ppermute | solution.py:23
  190.4 4.7 %shard_map.19 = f32[128,128]{1,0:T(8,128)} custom-call(f32[128,128]{1,0:T(8,128)} %fusion.28.g_ref), custom_call_target="tpu_custom_call" | custom-call | tf_op jit(solution)/shard_map/pallas_call | solution.py:80
  197.0 5.9 %fusion.24 = f32[128,8192]{1,0:T(8,128)S(1)} fusion(f32[128,128]{1,0:T(8,128)S(1)} %maximum_select_fusion.1, f32[64,8192]{1,0:T(8,128)} %copy-done.3, f32[64,8192]{1,0:T(8,128)S(1)} %get-tuple-element.25), kind=kOutput, calls=%fused_computation.28 | convolution fusion | flops 1611661312 | bytes 8454144 | tf_op jit(solution)/shard_map/in,ij->jn/dot_general | solution.py:213
  212.2 6.8 %collective-permute-start.4 = (f32[64,8192]{1,0:T(8,128)S(1)}, f32[64,8192]{1,0:T(8,128)S(1)}, u32[]{:S(2)}, u32[]{:S(2)}) collective-permute-start(f32[64,8192]{1,0:T(8,128)S(1)} %get-tuple-element.15), channel_id=1, source_target_pairs={{0,1},{1,2},{2,3},{3,4},{4,5},{5,6},{6,7},{7,8},{8,9},{9,10},{10,1... | collective-permute-start | bytes 6291464 | tf_op jit(solution)/shard_map/ppermute | solution.py:23
  221.3 7.0 %collective-permute-done.6 = f32[64,8192]{1,0:T(8,128)S(1)} collective-permute-done((f32[64,8192]{1,0:T(8,128)S(1)}, f32[64,8192]{1,0:T(8,128)S(1)}, u32[]{:S(2)}, u32[]{:S(2)}) %collective-permute-start.6) | collective-permute-done | bytes 2097184 | tf_op jit(solution)/shard_map/ppermute | solution.py:23
  228.3 8.0 %collective-permute-done.7 = f32[64,8192]{1,0:T(8,128)S(1)} collective-permute-done((f32[64,8192]{1,0:T(8,128)S(1)}, f32[64,8192]{1,0:T(8,128)S(1)}, u32[]{:S(2)}, u32[]{:S(2)}) %collective-permute-start.7) | collective-permute-done | bytes 2097184 | tf_op jit(solution)/shard_map/ppermute | solution.py:23
  240.2 10.6 %collective-permute-done.4 = f32[64,8192]{1,0:T(8,128)S(1)} collective-permute-done((f32[64,8192]{1,0:T(8,128)S(1)}, f32[64,8192]{1,0:T(8,128)S(1)}, u32[]{:S(2)}, u32[]{:S(2)}) %collective-permute-start.4) | collective-permute-done | bytes 2097184 | tf_op jit(solution)/shard_map/ppermute | solution.py:23
  250.8 8.0 %collective-permute-done.5 = f32[64,8192]{1,0:T(8,128)S(1)} collective-permute-done((f32[64,8192]{1,0:T(8,128)S(1)}, f32[64,8192]{1,0:T(8,128)S(1)}, u32[]{:S(2)}, u32[]{:S(2)}) %collective-permute-start.5) | collective-permute-done | bytes 2097184 | tf_op jit(solution)/shard_map/ppermute | solution.py:23
  265.5 4.7 %shard_map.20 = f32[128,128]{1,0:T(8,128)} custom-call(f32[128,128]{1,0:T(8,128)} %fusion.29.g_ref), custom_call_target="tpu_custom_call" | custom-call | tf_op jit(solution)/shard_map/pallas_call | solution.py:80
  272.1 5.8 %fusion.20 = f32[128,8192]{1,0:T(8,128)S(1)} fusion(f32[128,128]{1,0:T(8,128)S(1)} %maximum_select_fusion.2, f32[64,8192]{1,0:T(8,128)} %copy-done.4, f32[64,8192]{1,0:T(8,128)S(1)} %get-tuple-element.17), kind=kOutput, calls=%fused_computation.24 | convolution fusion | flops 1611661312 | bytes 8454144 | tf_op jit(solution)/shard_map/in,ij->jn/dot_general | solution.py:213
  287.3 6.8 %collective-permute-start.8 = (f32[64,8192]{1,0:T(8,128)S(1)}, f32[64,8192]{1,0:T(8,128)S(1)}, u32[]{:S(2)}, u32[]{:S(2)}) collective-permute-start(f32[64,8192]{1,0:T(8,128)S(1)} %get-tuple-element.7), channel_id=1, source_target_pairs={{0,1},{1,2},{2,3},{3,4},{4,5},{5,6},{6,7},{7,8},{8,9},{9,10},{10,1... | collective-permute-start | bytes 6291464 | tf_op jit(solution)/shard_map/ppermute | solution.py:23
  296.2 7.2 %collective-permute-done.10 = f32[64,8192]{1,0:T(8,128)S(1)} collective-permute-done((f32[64,8192]{1,0:T(8,128)S(1)}, f32[64,8192]{1,0:T(8,128)S(1)}, u32[]{:S(2)}, u32[]{:S(2)}) %collective-permute-start.10) | collective-permute-done | bytes 2097184 | tf_op jit(solution)/shard_map/ppermute | solution.py:23
  303.4 8.0 %collective-permute-done.11 = f32[64,8192]{1,0:T(8,128)S(1)} collective-permute-done((f32[64,8192]{1,0:T(8,128)S(1)}, f32[64,8192]{1,0:T(8,128)S(1)}, u32[]{:S(2)}, u32[]{:S(2)}) %collective-permute-start.11) | collective-permute-done | bytes 2097184 | tf_op jit(solution)/shard_map/ppermute | solution.py:23
  315.3 10.6 %collective-permute-done.8 = f32[64,8192]{1,0:T(8,128)S(1)} collective-permute-done((f32[64,8192]{1,0:T(8,128)S(1)}, f32[64,8192]{1,0:T(8,128)S(1)}, u32[]{:S(2)}, u32[]{:S(2)}) %collective-permute-start.8) | collective-permute-done | bytes 2097184 | tf_op jit(solution)/shard_map/ppermute | solution.py:23
  325.9 8.0 %collective-permute-done.9 = f32[64,8192]{1,0:T(8,128)S(1)} collective-permute-done((f32[64,8192]{1,0:T(8,128)S(1)}, f32[64,8192]{1,0:T(8,128)S(1)}, u32[]{:S(2)}, u32[]{:S(2)}) %collective-permute-start.9) | collective-permute-done | bytes 2097184 | tf_op jit(solution)/shard_map/ppermute | solution.py:23
  345.3 18.7 %fusion = f32[16384,128]{1,0:T(8,128)} fusion(f32[128,128]{1,0:T(8,128)} %shard_map.21, f32[64,8192]{1,0:T(8,128)} %copy-done.13, f32[64,8192]{1,0:T(8,128)S(1)} %get-tuple-element.9, f32[64,8192]{1,0:T(8,128)} %copy-done.15, f32[64,8192]{1,0:T(8,128)} %copy-done.14), kind=kOutput, calls=%fused_computation | convolution fusion | flops 3227516928 | bytes 16842752 | tf_op jit(solution)/shard_map/in,ij->nj/dot_general | solution.py:217
  (76 shorter events, 87.3 us)
Async XLA Ops:
  110.3 19.3 %slice-start = ((s8[8388608]{0:T(1024)(128)(4,1)}), s8[4194304]{0:T(1024)(128)(4,1)S(1)}, s32[]{:S(2)}) async-start(s8[8388608]{0:T(1024)(128)(4,1)} %bitcast.9), calls=%async_computation | async-start | bytes 8388608
  111.4 18.2 %slice-start.1 = ((s8[8388608]{0:T(1024)(128)(4,1)}), s8[4194304]{0:T(1024)(128)(4,1)S(1)}, s32[]{:S(2)}) async-start(s8[8388608]{0:T(1024)(128)(4,1)} %bitcast.9), calls=%async_computation.1 | async-start | bytes 8388608
  117.1 3.3 copy-start.2
  120.4 34.3 %collective-permute-start.2 = (f32[64,8192]{1,0:T(8,128)}, f32[64,8192]{1,0:T(8,128)S(1)}, u32[]{:S(2)}, u32[]{:S(2)}) collective-permute-start(f32[64,8192]{1,0:T(8,128)} %get-tuple-element.27), channel_id=1, source_target_pairs={{0,1},{1,2},{2,3},{3,4},{4,5},{5,6},{6,7},{7,8},{8,9},{9,10},{10,1... | collective-permute-start | bytes 6291464 | tf_op jit(solution)/shard_map/ppermute | solution.py:23
  127.7 31.3 %collective-permute-start.3 = (f32[64,8192]{1,0:T(8,128)}, f32[64,8192]{1,0:T(8,128)}, u32[]{:S(2)}, u32[]{:S(2)}) collective-permute-start(f32[64,8192]{1,0:T(8,128)} %get-tuple-element.28), channel_id=1, source_target_pairs={{1,0},{2,1},{3,2},{4,3},{5,4},{6,5},{7,6},{8,7},{9,8},{10,9},{11,1... | collective-permute-start | bytes 6291464 | tf_op jit(solution)/shard_map/ppermute | solution.py:23
  133.4 3.2 copy-start
  136.7 36.8 %collective-permute-start = (f32[64,8192]{1,0:T(8,128)}, f32[64,8192]{1,0:T(8,128)}, u32[]{:S(2)}, u32[]{:S(2)}) collective-permute-start(f32[64,8192]{1,0:T(8,128)} %get-tuple-element.23), channel_id=1, source_target_pairs={{0,1},{1,2},{2,3},{3,4},{4,5},{5,6},{6,7},{7,8},{8,9},{9,10},{10,1... | collective-permute-start | bytes 6291464 | tf_op jit(solution)/shard_map/ppermute | solution.py:23
  143.9 37.5 %collective-permute-start.1 = (f32[64,8192]{1,0:T(8,128)}, f32[64,8192]{1,0:T(8,128)}, u32[]{:S(2)}, u32[]{:S(2)}) collective-permute-start(f32[64,8192]{1,0:T(8,128)} %get-tuple-element.24), channel_id=1, source_target_pairs={{1,0},{2,1},{3,2},{4,3},{5,4},{6,5},{7,6},{8,7},{9,8},{10,9},{11,1... | collective-permute-start | bytes 6291464 | tf_op jit(solution)/shard_map/ppermute | solution.py:23
  162.9 3.4 copy-start.3
  162.9 18.6 %copy-start.1 = (f32[128,8192]{1,0:T(8,128)S(1)}, f32[128,8192]{1,0:T(8,128)}, u32[]{:S(2)}) copy-start(f32[128,8192]{1,0:T(8,128)} %copy-done) | copy-start | bytes 12582916
  202.9 4.9 %copy-start.6 = (f32[64,8192]{1,0:T(8,128)S(1)}, f32[64,8192]{1,0:T(8,128)}, u32[]{:S(2)}) copy-start(f32[64,8192]{1,0:T(8,128)} %copy-done.5) | copy-start | bytes 6291460
  202.9 4.9 %copy-start.8 = (f32[64,8192]{1,0:T(8,128)S(1)}, f32[64,8192]{1,0:T(8,128)}, u32[]{:S(2)}) copy-start(f32[64,8192]{1,0:T(8,128)} %copy-done.7) | copy-start | bytes 6291460
  203.2 25.1 %collective-permute-start.6 = (f32[64,8192]{1,0:T(8,128)S(1)}, f32[64,8192]{1,0:T(8,128)S(1)}, u32[]{:S(2)}, u32[]{:S(2)}) collective-permute-start(f32[64,8192]{1,0:T(8,128)S(1)} %get-tuple-element.19), channel_id=1, source_target_pairs={{0,1},{1,2},{2,3},{3,4},{4,5},{5,6},{6,7},{7,8},{8,9},{9,10},{10,1... | collective-permute-start | bytes 6291464 | tf_op jit(solution)/shard_map/ppermute | solution.py:23
  205.4 31.0 %collective-permute-start.7 = (f32[64,8192]{1,0:T(8,128)S(1)}, f32[64,8192]{1,0:T(8,128)S(1)}, u32[]{:S(2)}, u32[]{:S(2)}) collective-permute-start(f32[64,8192]{1,0:T(8,128)S(1)} %get-tuple-element.20), channel_id=1, source_target_pairs={{1,0},{2,1},{3,2},{4,3},{5,4},{6,5},{7,6},{8,7},{9,8},{10,9},{11,1... | collective-permute-start | bytes 6291464 | tf_op jit(solution)/shard_map/ppermute | solution.py:23
  212.2 38.6 %collective-permute-start.4 = (f32[64,8192]{1,0:T(8,128)S(1)}, f32[64,8192]{1,0:T(8,128)S(1)}, u32[]{:S(2)}, u32[]{:S(2)}) collective-permute-start(f32[64,8192]{1,0:T(8,128)S(1)} %get-tuple-element.15), channel_id=1, source_target_pairs={{0,1},{1,2},{2,3},{3,4},{4,5},{5,6},{6,7},{7,8},{8,9},{9,10},{10,1... | collective-permute-start | bytes 6291464 | tf_op jit(solution)/shard_map/ppermute | solution.py:23
  219.0 39.8 %collective-permute-start.5 = (f32[64,8192]{1,0:T(8,128)S(1)}, f32[64,8192]{1,0:T(8,128)S(1)}, u32[]{:S(2)}, u32[]{:S(2)}) collective-permute-start(f32[64,8192]{1,0:T(8,128)S(1)} %get-tuple-element.16), channel_id=1, source_target_pairs={{1,0},{2,1},{3,2},{4,3},{5,4},{6,5},{7,6},{8,7},{9,8},{10,9},{11,1... | collective-permute-start | bytes 6291464 | tf_op jit(solution)/shard_map/ppermute | solution.py:23
  236.8 3.4 copy-start.4
  277.9 4.9 %copy-start.10 = (f32[64,8192]{1,0:T(8,128)S(1)}, f32[64,8192]{1,0:T(8,128)}, u32[]{:S(2)}) copy-start(f32[64,8192]{1,0:T(8,128)} %copy-done.9) | copy-start | bytes 6291460
  278.0 4.9 %copy-start.12 = (f32[64,8192]{1,0:T(8,128)S(1)}, f32[64,8192]{1,0:T(8,128)}, u32[]{:S(2)}) copy-start(f32[64,8192]{1,0:T(8,128)} %copy-done.11) | copy-start | bytes 6291460
  278.2 25.1 %collective-permute-start.10 = (f32[64,8192]{1,0:T(8,128)S(1)}, f32[64,8192]{1,0:T(8,128)S(1)}, u32[]{:S(2)}, u32[]{:S(2)}) collective-permute-start(f32[64,8192]{1,0:T(8,128)S(1)} %get-tuple-element.11), channel_id=1, source_target_pairs={{0,1},{1,2},{2,3},{3,4},{4,5},{5,6},{6,7},{7,8},{8,9},{9,10},{10,1... | collective-permute-start | bytes 6291464 | tf_op jit(solution)/shard_map/ppermute | solution.py:23
  280.4 31.0 %collective-permute-start.11 = (f32[64,8192]{1,0:T(8,128)S(1)}, f32[64,8192]{1,0:T(8,128)S(1)}, u32[]{:S(2)}, u32[]{:S(2)}) collective-permute-start(f32[64,8192]{1,0:T(8,128)S(1)} %get-tuple-element.12), channel_id=1, source_target_pairs={{1,0},{2,1},{3,2},{4,3},{5,4},{6,5},{7,6},{8,7},{9,8},{10,9},{11,1... | collective-permute-start | bytes 6291464 | tf_op jit(solution)/shard_map/ppermute | solution.py:23
  287.3 38.6 %collective-permute-start.8 = (f32[64,8192]{1,0:T(8,128)S(1)}, f32[64,8192]{1,0:T(8,128)S(1)}, u32[]{:S(2)}, u32[]{:S(2)}) collective-permute-start(f32[64,8192]{1,0:T(8,128)S(1)} %get-tuple-element.7), channel_id=1, source_target_pairs={{0,1},{1,2},{2,3},{3,4},{4,5},{5,6},{6,7},{7,8},{8,9},{9,10},{10,1... | collective-permute-start | bytes 6291464 | tf_op jit(solution)/shard_map/ppermute | solution.py:23
  294.1 39.8 %collective-permute-start.9 = (f32[64,8192]{1,0:T(8,128)S(1)}, f32[64,8192]{1,0:T(8,128)S(1)}, u32[]{:S(2)}, u32[]{:S(2)}) collective-permute-start(f32[64,8192]{1,0:T(8,128)S(1)} %get-tuple-element.8), channel_id=1, source_target_pairs={{1,0},{2,1},{3,2},{4,3},{5,4},{6,5},{7,6},{8,7},{9,8},{10,9},{11,1... | collective-permute-start | bytes 6291464 | tf_op jit(solution)/shard_map/ppermute | solution.py:23
  311.8 3.4 copy-start.13
  (7 other events, 11.4 us)
